TPU v7x, 128 devices: a whole 4x4x4 slice. The times are simulated.
128 devices in a mesh: req: 32 (over z_hi, x, y), tp: 4 (over z_lo, core).
Axes of the slice: x: 4, y: 4, z: 4 (z_hi: 2, z_lo: 2; z = z_hi * 2 + z_lo), core: 2. Of those that a mesh axis runs over, the one named last changes fastest.
Arguments:
- hidden_in: bfloat16 [65536, 1024], P('req'), may hold values from -6 to 6
- lengths: int32 [64], replicated, may hold values from 1 to 2048, 65536 in all
- tenant: int32 [64], replicated, may hold values from 0 to 3
- shard_map: int32 [128], replicated, may hold values from 0 to 127, each once
- wq: float32 [1024, 1024], P(('req', 'tp')), as said below
- wk: float32 [1024, 1024], P(('req', 'tp')), as said below
- wv: float32 [1024, 1024], P(('req', 'tp')), may hold values from -0.75 to 0.75
- wo: float32 [1024, 1024], P(('req', 'tp')), may hold values from -0.75 to 0.75
- wi_in: float32 [1024, 2624], P(('req', 'tp')), may hold values from -0.1875 to 0.1875
- wi_gate: float32 [1024, 2624], P(('req', 'tp')), may hold values from -0.1875 to 0.1875
- wo2: float32 [1024, 2624], P(('req', 'tp')), may hold values from -0.125 to 0.125
- head: float32 [49152, 1024], P(('req', 'tp')), may hold values from -0.56 to 0.56
- attn_gain: float32 [1024], replicated, may hold values from 0.1 to 1.9
- mlp_gain: float32 [1024], replicated, may hold values from 0.1 to 1.9
- final_gain: float32 [4, 1024], replicated, may hold values from 0.1 to 1.9
Outputs:
- hidden_out: bfloat16 [65536, 1024], P('req', 'tp')
- cache: bfloat16 [2, 65536, 1024], P(None, 'req', 'tp')
- last_rms: float32 [64], replicated
- top_logit: float32 [64], replicated
Inputs may be any that keep to these rules, and one draw needn't show every extreme that they name: Prompts are packed in request order into the 65536 slots; the lengths sum to 65536 and the longest is exactly 2048. `shard_map`: A permutation: each row block is held by exactly one trainer device. `wq`: A fan-in scaled projection. `wk`: A fan-in scaled projection.
All inputs are finite; a program needn't handle non-finite values.
Results may differ from a plain program's by a relative error of at most 0.012.
The roundings to bfloat16 on the way count: a program that leaves them out, or rounds other values in their place, can miss the bound.
Values may be sent and summed in bfloat16 or wider, within the bound.
No kernel may reach another device: no remote copies, remote signals or barrier semaphores. Data moves between devices by JAX's collectives and lax.ppermute only.
A program may use at most 128 MiB of HBM per device.

v0:
```python
import jax
import jax.numpy as jnp
from jax import lax
from jax.sharding import PartitionSpec as P

HEADS = 16
HEAD_DIM = 64
THETA = 160000.0
EPS = 1e-05


def with_halo(block, sides, width):
    for axis, dim in sides:
        count = lax.axis_size(axis)
        forward = [(i, i + 1) for i in range(count - 1)]
        backward = [(target, source) for source, target in forward]
        low = lax.ppermute(
            lax.slice_in_dim(block, block.shape[dim] - width, None, axis=dim), axis, forward
        )
        high = lax.ppermute(lax.slice_in_dim(block, 0, width, axis=dim), axis, backward)
        block = jnp.concatenate([low, block, high], axis=dim)
    return block


def layer_norm(values, gain):
    center = jnp.mean(values, axis=-1, keepdims=True)
    spread = jnp.mean(values * values, axis=-1, keepdims=True) - center * center
    return (values - center) * lax.rsqrt(spread + EPS) * gain


def rotate(values, position):
    half = values.shape[-1] // 2
    freq = THETA ** (-(2.0 * jnp.arange(half, dtype=jnp.float32)) / values.shape[-1])
    angle = position.astype(jnp.float32)[:, None] * freq[None, :]
    cosine = jnp.cos(angle)[:, None, :]
    sine = jnp.sin(angle)[:, None, :]
    first = values[..., :half]
    second = values[..., half:]
    return jnp.concatenate(
        [first * cosine - second * sine, second * cosine + first * sine], axis=-1
    )


def reorder(weight, holder, shard_map, count):
    block_of = shard_map[holder]
    order = jnp.zeros((count,), jnp.int32).at[block_of].set(jnp.arange(count, dtype=jnp.int32))
    rows = weight.shape[0] // count
    return weight.reshape(count, rows, weight.shape[1])[order].reshape(
        weight.shape[0], weight.shape[1]
    )


def body(
    hidden_in,
    lengths,
    tenant,
    shard_map,
    wq,
    wk,
    wv,
    wo,
    wi_in,
    wi_gate,
    wo2,
    head,
    attn_gain,
    mlp_gain,
    final_gain,
):
    req_count = lax.axis_size("req")
    tp_count = lax.axis_size("tp")
    count = req_count * tp_count
    req_index = lax.axis_index("req")
    tp_index = lax.axis_index("tp")
    slots, width = hidden_in.shape
    local_heads = HEADS // tp_count
    share = width // tp_count
    served = (
        wq.astype(jnp.bfloat16),
        wk.astype(jnp.bfloat16),
        wv.astype(jnp.bfloat16),
        wo.astype(jnp.bfloat16),
        wi_in.astype(jnp.bfloat16),
        wi_gate.astype(jnp.bfloat16),
        wo2.astype(jnp.bfloat16),
    )
    place = jnp.arange(count, dtype=jnp.int32)
    collected = (
        lax.all_gather(served[0], "req", axis=0, tiled=True),
        lax.all_gather(served[1], "req", axis=0, tiled=True),
        lax.all_gather(served[2], "req", axis=0, tiled=True),
        lax.all_gather(served[3], "req", axis=0, tiled=True),
        lax.all_gather(served[4], "req", axis=0, tiled=True),
        lax.all_gather(served[5], "req", axis=0, tiled=True),
        lax.all_gather(served[6], "req", axis=0, tiled=True),
    )
    regrouped = (
        lax.all_to_all(collected[0], "tp", split_axis=1, concat_axis=0, tiled=True),
        lax.all_to_all(collected[1], "tp", split_axis=1, concat_axis=0, tiled=True),
        lax.all_to_all(collected[2], "tp", split_axis=1, concat_axis=0, tiled=True),
        lax.all_to_all(collected[3], "tp", split_axis=1, concat_axis=0, tiled=True),
        lax.all_to_all(collected[4], "tp", split_axis=1, concat_axis=0, tiled=True),
        lax.all_to_all(collected[5], "tp", split_axis=1, concat_axis=0, tiled=True),
        lax.all_to_all(collected[6], "tp", split_axis=1, concat_axis=0, tiled=True),
    )
    holder = place % req_count * tp_count + place // req_count
    query_w, key_w, value_w, out_w, input_w, gate_w, down_w = [
        reorder(item, holder, shard_map, count) for item in regrouped
    ]
    ends = jnp.cumsum(lengths)
    total = slots * req_count
    base = req_index * slots
    global_index = base - slots + jnp.arange(3 * slots, dtype=jnp.int32)
    before = ends[None, :] <= global_index[:, None]
    segment = jnp.sum(before.astype(jnp.int32), axis=1)
    inside = (global_index >= 0) & (global_index < total)
    segment = jnp.where(inside, segment, -1)
    own_segment = segment[slots : 2 * slots]
    own_index = global_index[slots : 2 * slots]
    own_before = before[slots : 2 * slots]
    position = own_index - jnp.sum(jnp.where(own_before, lengths[None, :], 0), axis=1)
    normed = layer_norm(hidden_in.astype(jnp.float32), attn_gain).astype(jnp.bfloat16)
    query = jnp.dot(normed, query_w, preferred_element_type=jnp.float32).reshape(
        slots, local_heads, HEAD_DIM
    )
    query = rotate(query, position).astype(jnp.bfloat16)
    keys = jnp.dot(normed, key_w, preferred_element_type=jnp.float32).reshape(
        slots, local_heads, HEAD_DIM
    )
    keys = rotate(keys, position).astype(jnp.bfloat16).reshape(slots, share)
    values = jnp.dot(normed, value_w, preferred_element_type=jnp.float32).astype(jnp.bfloat16)
    cache = jnp.stack([keys, values])
    widened = with_halo(cache, (("req", 1),), slots)
    key_heads = widened[0].reshape(3 * slots, local_heads, HEAD_DIM).transpose(1, 0, 2)
    value_heads = widened[1].reshape(3 * slots, local_heads, HEAD_DIM).transpose(1, 0, 2)
    query_heads = query.transpose(1, 0, 2)
    block = min(512, slots)
    scale = HEAD_DIM ** (-0.5)

    def head_attend(operands):
        query_head, key_head, value_head = operands

        def one_block(number):
            start = number * block
            query_block = lax.dynamic_slice_in_dim(query_head, start, block, 0)
            query_segment = lax.dynamic_slice_in_dim(own_segment, start, block, 0)
            scores = (
                lax.dot_general(
                    query_block,
                    key_head,
                    (((1,), (1,)), ((), ())),
                    preferred_element_type=jnp.float32,
                )
                * scale
            )
            scores = jnp.where(query_segment[:, None] == segment[None, :], scores, -1e30)
            highest = jnp.max(scores, axis=-1, keepdims=True)
            weights = jnp.exp(scores - highest)
            probability = (weights / jnp.sum(weights, axis=-1, keepdims=True)).astype(jnp.bfloat16)
            return jnp.dot(probability, value_head, preferred_element_type=jnp.float32)

        result = lax.map(one_block, jnp.arange(slots // block, dtype=jnp.int32))
        return result.reshape(slots, HEAD_DIM)

    attended = lax.map(head_attend, (query_heads, key_heads, value_heads))
    mixed = attended.transpose(1, 0, 2).reshape(slots, share).astype(jnp.bfloat16)
    attn_part = lax.dot_general(
        mixed, out_w, (((1,), (1,)), ((), ())), preferred_element_type=jnp.float32
    )
    summed = lax.psum(attn_part, "tp")
    first = (hidden_in.astype(jnp.float32) + summed).astype(jnp.bfloat16)
    normed2 = layer_norm(first.astype(jnp.float32), mlp_gain).astype(jnp.bfloat16)
    first_share = lax.dynamic_slice_in_dim(first, tp_index * share, share, 1)
    gate_in = jnp.dot(normed2, input_w, preferred_element_type=jnp.float32)
    gate_side = jnp.dot(normed2, gate_w, preferred_element_type=jnp.float32)
    inner = (jax.nn.gelu(gate_in, approximate=False) * gate_side).astype(jnp.bfloat16)
    down_part = lax.dot_general(
        inner, down_w, (((1,), (1,)), ((), ())), preferred_element_type=jnp.float32
    )
    down_share = lax.psum_scatter(down_part, "tp", scatter_dimension=1, tiled=True)
    hidden_out = (first_share.astype(jnp.float32) + down_share).astype(jnp.bfloat16)
    last_slot = ends - 1 - base
    holds = (last_slot >= 0) & (last_slot < slots)
    picked = hidden_out[jnp.clip(last_slot, 0, slots - 1)].astype(jnp.float32)
    picked = jnp.where(holds[:, None], picked, 0.0)
    request_count = lengths.shape[0]
    placed = lax.dynamic_update_slice(
        jnp.zeros((request_count, width), jnp.float32), picked, (jnp.int32(0), tp_index * share)
    )
    last = lax.psum(placed, ("req", "tp"))
    last_rms = jnp.sqrt(jnp.mean(last * last, axis=-1))
    choose = (tenant[:, None] == jnp.arange(final_gain.shape[0], dtype=jnp.int32)[None, :]).astype(
        jnp.float32
    )
    gain_rows = jnp.dot(
        choose, final_gain, precision=lax.Precision.HIGHEST, preferred_element_type=jnp.float32
    )
    final = layer_norm(last, gain_rows).astype(jnp.bfloat16)
    logits = lax.dot_general(
        final,
        head.astype(jnp.bfloat16),
        (((1,), (1,)), ((), ())),
        preferred_element_type=jnp.float32,
    )
    top_logit = lax.pmax(jnp.max(logits, axis=-1), ("req", "tp"))
    return (hidden_out, cache, last_rms, top_logit)


def solution(mesh):
    placed = (
        P("req", None),
        P(),
        P(),
        P(),
        P(("req", "tp"), None),
        P(("req", "tp"), None),
        P(("req", "tp"), None),
        P(("req", "tp"), None),
        P(("req", "tp"), None),
        P(("req", "tp"), None),
        P(("req", "tp"), None),
        P(("req", "tp"), None),
        P(),
        P(),
        P(),
    )
    return jax.shard_map(
        body,
        mesh=mesh,
        in_specs=placed,
        out_specs=(P("req", "tp"), P(None, "req", "tp"), P(), P()),
        check_vma=False,
    )
```

profile of v0, /device:TPU:1, one launch (start us, length us, event | category | flops | bytes accessed | tf_op | source)
XLA Modules:
  0.0 1209.6 jit_solution(8971452301709203540)
XLA Ops:
  10.4 85.3 %all_gather.22 = bf16[256,1024]{1,0:T(8,128)(2,1)S(1)} all-gather(bf16[8,1024]{1,0:T(8,128)(2,1)S(1)} %convert_element_type.94), channel_id=1, replica_groups=mesh['req'=32,'tp'=4] {'req'}, dimensions={0}, use_global_device_ids=true | all-gather | bytes 540672 | tf_op jit(solution)/shard_map/all_gather | solution.py:90
  96.7 18.5 %all-to-all-start.1 = ((bf16[256,4,256]{0,2,1:T(8,128)(2,1)}), bf16[256,4,256]{0,2,1:T(8,128)(2,1)S(1)}, u32[]{:S(2)}, u32[]{:S(2)}) async-start(bf16[256,4,256]{0,2,1:T(8,128)(2,1)} %bitcast.18), calls=%async_computation.1 | async-start | bytes 1048576 | tf_op jit(solution)/shard_map/all_to_all | solution.py:99
  124.0 76.5 %all_gather.21 = bf16[256,1024]{1,0:T(8,128)(2,1)S(1)} all-gather(bf16[8,1024]{1,0:T(8,128)(2,1)S(1)} %convert_element_type.92), channel_id=1, replica_groups=mesh['req'=32,'tp'=4] {'req'}, dimensions={0}, use_global_device_ids=true | all-gather | bytes 540672 | tf_op jit(solution)/shard_map/all_gather | solution.py:89
  200.5 78.2 %all_gather.23 = bf16[256,1024]{1,0:T(8,128)(2,1)S(1)} all-gather(bf16[8,1024]{1,0:T(8,128)(2,1)S(1)} %convert_element_type.96), channel_id=1, replica_groups=mesh['req'=32,'tp'=4] {'req'}, dimensions={0}, use_global_device_ids=true | all-gather | bytes 540672 | tf_op jit(solution)/shard_map/all_gather | solution.py:91
  279.0 4.3 fusion.12
  285.6 31.4 %all-to-all-start = ((bf16[256,4,256]{0,2,1:T(8,128)(2,1)}), bf16[256,4,256]{0,2,1:T(8,128)(2,1)S(1)}, u32[]{:S(2)}, u32[]{:S(2)}) async-start(bf16[256,4,256]{0,2,1:T(8,128)(2,1)} %bitcast.7), calls=%async_computation | async-start | bytes 1048576 | tf_op jit(solution)/shard_map/all_to_all | solution.py:98
  319.0 5.9 all-to-all-done
  325.0 4.8 all-to-all-start.2
  330.8 3.7 fusion.26
  347.1 114.9 %all_gather.24 = bf16[256,1024]{1,0:T(8,128)(2,1)S(1)} all-gather(bf16[8,1024]{1,0:T(8,128)(2,1)S(1)} %convert_element_type.102), channel_id=1, replica_groups=mesh['req'=32,'tp'=4] {'req'}, dimensions={0}, use_global_device_ids=true | all-gather | bytes 540672 | tf_op jit(solution)/shard_map/all_gather | solution.py:92
  463.0 17.3 %all-to-all-start.3 = ((bf16[256,4,256]{0,2,1:T(8,128)(2,1)}), bf16[256,4,256]{0,2,1:T(8,128)(2,1)S(1)}, u32[]{:S(2)}, u32[]{:S(2)}) async-start(bf16[256,4,256]{0,2,1:T(8,128)(2,1)} %bitcast.36), calls=%async_computation.3 | async-start | bytes 1048576 | tf_op jit(solution)/shard_map/all_to_all | solution.py:101
  481.6 6.9 all-to-all-done.3
  496.5 4.8 copy.103
  504.5 160.4 %while.21 = (s32[]{:T(128)}, bf16[4,2048,64]{1,2,0:T(8,128)(2,1)}, bf16[4,2048,64]{1,2,0:T(8,128)(2,1)}, bf16[4,6144,64]{1,2,0:T(8,128)(2,1)}, bf16[4,6144,64]{1...) while((s32[]{:T(128)}, bf16[4,2048,64]{1,2,0:T(8,128)(2,1)}, ...), condition=%wide.region_11.12_spmd, body=%wide.region_6.0_spmd.sunk | while | flops 833616896 | bytes 53257172 | solution.py:165
  509.6 33.7 %while.22 = (s32[]{:T(128)}, bf16[4,512,64]{1,2,0:T(8,128)(2,1)S(1)}, s32[4]{0:T(128)S(1)}, s32[2048]{0:T(1024)S(1)}, s32[6144]{0:T(1024)S(1)}, /*index=5*/bf16[...) while((s32[]{:T(128)}, ...), condition=%wide.region_10.10_spmd, body=%wide.region_7.9_spmd.sunk | while | flops 833616896 | bytes 44343512 | solution.py:162
  549.7 33.7 %while.22 = (s32[]{:T(128)}, bf16[4,512,64]{1,2,0:T(8,128)(2,1)S(1)}, s32[4]{0:T(128)S(1)}, s32[2048]{0:T(1024)S(1)}, s32[6144]{0:T(1024)S(1)}, /*index=5*/bf16[...) while((s32[]{:T(128)}, ...), condition=%wide.region_10.10_spmd, body=%wide.region_7.9_spmd.sunk | while | flops 833616896 | bytes 44343512 | solution.py:162
  589.8 33.7 %while.22 = (s32[]{:T(128)}, bf16[4,512,64]{1,2,0:T(8,128)(2,1)S(1)}, s32[4]{0:T(128)S(1)}, s32[2048]{0:T(1024)S(1)}, s32[6144]{0:T(1024)S(1)}, /*index=5*/bf16[...) while((s32[]{:T(128)}, ...), condition=%wide.region_10.10_spmd, body=%wide.region_7.9_spmd.sunk | while | flops 833616896 | bytes 44343512 | solution.py:162
  629.9 33.7 %while.22 = (s32[]{:T(128)}, bf16[4,512,64]{1,2,0:T(8,128)(2,1)S(1)}, s32[4]{0:T(128)S(1)}, s32[2048]{0:T(1024)S(1)}, s32[6144]{0:T(1024)S(1)}, /*index=5*/bf16[...) while((s32[]{:T(128)}, ...), condition=%wide.region_10.10_spmd, body=%wide.region_7.9_spmd.sunk | while | flops 833616896 | bytes 44343512 | solution.py:162
  664.8 5.9 fusion.69
  673.3 4.4 all-to-all-start.4
  680.2 21.4 %all-to-all-done.4 = bf16[256,4,656]{0,2,1:T(8,128)(2,1)S(1)} async-done(((bf16[256,4,656]{0,2,1:T(8,128)(2,1)}), bf16[256,4,656]{0,2,1:T(8,128)(2,1)S(1)}, u32[]{:S(2)}, u32[]{:S(2)}) %all-to-all-start.4) | async-done | bytes 1343520 | tf_op jit(solution)/shard_map/all_to_all | solution.py:102
  701.6 5.2 all-to-all-start.5
  709.3 29.3 %all-to-all-done.5 = bf16[256,4,656]{0,2,1:T(8,128)(2,1)S(1)} async-done(((bf16[256,4,656]{0,2,1:T(8,128)(2,1)}), bf16[256,4,656]{0,2,1:T(8,128)(2,1)S(1)}, u32[]{:S(2)}, u32[]{:S(2)}) %all-to-all-start.5) | async-done | bytes 1343520 | tf_op jit(solution)/shard_map/all_to_all | solution.py:103
  738.6 5.0 all-to-all-start.6
  748.8 26.2 %all-to-all-done.6 = bf16[256,4,656]{0,2,1:T(8,128)(2,1)} async-done(((bf16[256,4,656]{0,2,1:T(8,128)(2,1)}), bf16[256,4,656]{0,2,1:T(8,128)(2,1)}, u32[]{:S(2)}, u32[]{:S(2)}) %all-to-all-start.6) | async-done | bytes 1343520 | tf_op jit(solution)/shard_map/all_to_all | solution.py:104
  778.7 95.2 %all-reduce.3.cloned.1.call-done = f32[2048,1024]{1,0:T(8,128)} async-done(((f32[2048,1024]{1,0:T(8,128)}), f32[2048,1024]{1,0:T(8,128)}) %all-reduce.3.cloned.1.call-update) | async-done | bytes 8388624 | tf_op jit(solution)/shard_map/psum | solution.py:170
  873.8 5.5 convert_reduce_fusion.1
  881.3 5.4 fusion.65
  886.7 23.0 %fusion.30 = f32[2048,1024]{1,0:T(8,128)} fusion(f32[2048,656]{0,1:T(8,128)} %fusion.65, bf16[128,8,656]{2,1,0:T(8,128)(2,1)} %gather_fusion.7, bf16[128,8,656]{2,1,0:T(8,128)(2,1)S(1)} %copy-done.12, bf16[2048,1024]{1,0:T(8,128)(2,1)} %copy-done.5, f32[1024]{0:T(1024)S(1)} %copy-done.25, f32[2048]{0:T(1024)S(1)} %get-tuple-element.173, ...), kind=kOutput, calls=%fused_computation.64 | convolution fusion | flops 5602082816 | bytes 20664320 | tf_op jit(solution)/shard_map/dot_general | solution.py:177
  910.4 79.1 %reduce-scatter.2.cloned.1.call-done = f32[2048,256]{1,0:T(8,128)} async-done(((f32[2048,1024]{1,0:T(8,128)}), f32[2048,256]{1,0:T(8,128)}) %reduce-scatter.2.cloned.1.call-update) | async-done | bytes 2097168 | tf_op jit(solution)/shard_map/reduce_scatter | solution.py:180
  993.2 142.3 %all-reduce.5.cloned.1.call-done = f32[64,1024]{1,0:T(8,128)} async-done(((f32[64,1024]{1,0:T(8,128)}), f32[64,1024]{1,0:T(8,128)}) %all-reduce.5.cloned.1.call-update) | async-done | bytes 262160 | tf_op jit(solution)/shard_map/psum | solution.py:190
  1138.9 63.4 %pmax.7 = f32[64]{0:T(128)} all-reduce(f32[64]{0:T(128)S(1)} %convolution_reduce_fusion), channel_id=1, replica_groups=mesh['req'=32,'tp'=4] {'req','tp'}, use_global_device_ids=true, to_apply=%region_20.21 | all-reduce | flops 64 | bytes 512 | tf_op jit(solution)/shard_map/pmax | solution.py:205
  (296 shorter events, 218.9 us)
Async XLA Ops:
  8.0 1129.1 %copy-start = (f32[4,1024]{1,0:T(4,128)S(1)}, f32[4,1024]{1,0:T(4,128)}, u32[]{:S(2)}) copy-start(f32[4,1024]{1,0:T(4,128)} %param.33) | copy-start | bytes 49156
  8.0 113.7 %copy-start.1 = (s32[128]{0:T(128)S(1)}, s32[128]{0:T(128)}, u32[]{:S(2)}) copy-start(s32[128]{0:T(128)} %param.22) | copy-start | bytes 1540
  8.0 115.9 %copy-start.15 = (f32[8,1024]{1,0:T(8,128)S(1)}, f32[8,1024]{1,0:T(8,128)}, u32[]{:S(2)}) copy-start(f32[8,1024]{1,0:T(8,128)} %param.23) | copy-start | bytes 98308
  8.0 192.4 %copy-start.16 = (f32[8,1024]{1,0:T(8,128)S(1)}, f32[8,1024]{1,0:T(8,128)}, u32[]{:S(2)}) copy-start(f32[8,1024]{1,0:T(8,128)} %param.25) | copy-start | bytes 98308
  8.0 271.0 %copy-start.21 = (f32[1024]{0:T(1024)S(1)}, f32[1024]{0:T(1024)}, u32[]{:S(2)}) copy-start(f32[1024]{0:T(1024)} %param.31) | copy-start | bytes 12292
  8.1 662.7 %all-gather.4.cloned.1.call-start = ((), (), s32[]{:S(2)}) async-start(), calls=%async_computation.9 | async-start | bytes 1419264 | tf_op jit(solution)/shard_map/all_gather | solution.py:93
  96.7 188.8 %all-to-all-start.1 = ((bf16[256,4,256]{0,2,1:T(8,128)(2,1)}), bf16[256,4,256]{0,2,1:T(8,128)(2,1)S(1)}, u32[]{:S(2)}, u32[]{:S(2)}) async-start(bf16[256,4,256]{0,2,1:T(8,128)(2,1)} %bitcast.18), calls=%async_computation.1 | async-start | bytes 1048576 | tf_op jit(solution)/shard_map/all_to_all | solution.py:99
  115.2 562.5 %all-gather.6.cloned.1.call-start = ((), (), s32[]{:S(2)}) async-start(), calls=%async_computation.10 | async-start | bytes 1419264 | tf_op jit(solution)/shard_map/all_gather | solution.py:94
  118.2 363.1 %copy-start.19 = (s32[64]{0:T(128)}, s32[64]{0:T(128)S(1)}, u32[]{:S(2)}) copy-start(s32[64]{0:T(128)S(1)} %get-tuple-element.126) | copy-start | bytes 772
  124.0 364.7 %copy-start.18 = (s32[1024]{0:T(1024)}, s32[1024]{0:T(1024)S(1)}, u32[]{:S(2)}) copy-start(s32[1024]{0:T(1024)S(1)} %pad_clamp_fusion.1) | copy-start | bytes 12292
  279.0 6.4 copy-start.22
  285.6 39.4 %all-to-all-start = ((bf16[256,4,256]{0,2,1:T(8,128)(2,1)}), bf16[256,4,256]{0,2,1:T(8,128)(2,1)S(1)}, u32[]{:S(2)}, u32[]{:S(2)}) async-start(bf16[256,4,256]{0,2,1:T(8,128)(2,1)} %bitcast.7), calls=%async_computation | async-start | bytes 1048576 | tf_op jit(solution)/shard_map/all_to_all | solution.py:98
  325.0 13.3 %all-to-all-start.2 = ((bf16[256,4,256]{0,2,1:T(8,128)(2,1)}), bf16[256,4,256]{0,2,1:T(8,128)(2,1)S(1)}, u32[]{:S(2)}, u32[]{:S(2)}) async-start(bf16[256,4,256]{0,2,1:T(8,128)(2,1)} %bitcast.25), calls=%async_computation.2 | async-start | bytes 1048576 | tf_op jit(solution)/shard_map/all_to_all | solution.py:100
  339.1 7.9 copy-start.17
  342.6 137.7 %copy-start.14 = (f32[8,2624]{1,0:T(8,128)S(1)}, f32[8,2624]{1,0:T(8,128)}, u32[]{:S(2)}) copy-start(f32[8,2624]{1,0:T(8,128)} %param.29) | copy-start | bytes 251908
  342.8 147.3 %copy-start.9 = (bf16[2,2048,256]{2,1,0:T(8,128)(2,1)}, bf16[2,2048,256]{2,1,0:T(8,128)(2,1)S(1)}, u32[]{:S(2)}) copy-start(bf16[2,2048,256]{2,1,0:T(8,128)(2,1)S(1)} %pad_maximum_fusion.1) | copy-start | bytes 6291460
  342.8 147.3 %collective-permute-start = (bf16[2,2048,256]{2,1,0:T(8,128)(2,1)S(1)}, bf16[2,2048,256]{2,1,0:T(8,128)(2,1)}, u32[]{:S(2)}, u32[]{:S(2)}) collective-permute-start(bf16[2,2048,256]{2,1,0:T(8,128)(2,1)S(1)} %pad_maximum_fusion.1), channel_id=1, source_target_pairs={{0,4},{4,8},{8,12},{12,16},{16,20},{20,24},{24,28},{28,32},{32,36}... | collective-permute-start | bytes 6291464 | tf_op jit(solution)/shard_map/ppermute | solution.py:17
  345.7 144.4 %collective-permute-start.1 = (bf16[2,2048,256]{2,1,0:T(8,128)(2,1)S(1)}, bf16[2,2048,256]{2,1,0:T(8,128)(2,1)}, u32[]{:S(2)}, u32[]{:S(2)}) collective-permute-start(bf16[2,2048,256]{2,1,0:T(8,128)(2,1)S(1)} %pad_maximum_fusion.1), channel_id=1, source_target_pairs={{4,0},{8,4},{12,8},{16,12},{20,16},{24,20},{28,24},{32,28},{36,32}... | collective-permute-start | bytes 6291464 | tf_op jit(solution)/shard_map/ppermute | solution.py:20
  463.0 25.5 %all-to-all-start.3 = ((bf16[256,4,256]{0,2,1:T(8,128)(2,1)}), bf16[256,4,256]{0,2,1:T(8,128)(2,1)S(1)}, u32[]{:S(2)}, u32[]{:S(2)}) async-start(bf16[256,4,256]{0,2,1:T(8,128)(2,1)} %bitcast.36), calls=%async_computation.3 | async-start | bytes 1048576 | tf_op jit(solution)/shard_map/all_to_all | solution.py:101
  480.3 226.5 %all-gather.8.cloned.1.call-start = ((), (), s32[]{:S(2)}) async-start(), calls=%async_computation.11 | async-start | bytes 1419264 | tf_op jit(solution)/shard_map/all_gather | solution.py:95
  481.0 392.8 %all-reduce.3.cloned.1.call-start = ((), (), s32[]{:S(2)}) async-start(), calls=%async_computation.8 | async-start | bytes 16777216 | tf_op jit(solution)/shard_map/psum | solution.py:170
  673.3 28.3 %all-to-all-start.4 = ((bf16[256,4,656]{0,2,1:T(8,128)(2,1)}), bf16[256,4,656]{0,2,1:T(8,128)(2,1)S(1)}, u32[]{:S(2)}, u32[]{:S(2)}) async-start(bf16[256,4,656]{0,2,1:T(8,128)(2,1)} %bitcast.40), calls=%async_computation.4 | async-start | bytes 2686976 | tf_op jit(solution)/shard_map/all_to_all | solution.py:102
  701.6 37.0 %all-to-all-start.5 = ((bf16[256,4,656]{0,2,1:T(8,128)(2,1)}), bf16[256,4,656]{0,2,1:T(8,128)(2,1)S(1)}, u32[]{:S(2)}, u32[]{:S(2)}) async-start(bf16[256,4,656]{0,2,1:T(8,128)(2,1)} %bitcast.116), calls=%async_computation.5 | async-start | bytes 2686976 | tf_op jit(solution)/shard_map/all_to_all | solution.py:103
  738.6 5.2 copy-start.6
  738.6 36.5 %all-to-all-start.6 = ((bf16[256,4,656]{0,2,1:T(8,128)(2,1)}), bf16[256,4,656]{0,2,1:T(8,128)(2,1)}, u32[]{:S(2)}, u32[]{:S(2)}) async-start(bf16[256,4,656]{0,2,1:T(8,128)(2,1)} %bitcast.115), calls=%async_computation.6 | async-start | bytes 2686976 | tf_op jit(solution)/shard_map/all_to_all | solution.py:104
  743.5 246.0 %reduce-scatter.2.cloned.1.call-start = ((), (), s32[]{:S(2)}) async-start(), calls=%async_computation.12 | async-start | bytes 10485760 | tf_op jit(solution)/shard_map/reduce_scatter | solution.py:180
  778.7 102.7 %copy-start.25 = (f32[1024]{0:T(1024)S(1)}, f32[1024]{0:T(1024)}, u32[]{:S(2)}) copy-start(f32[1024]{0:T(1024)} %param.32) | copy-start | bytes 12292
  881.3 5.4 copy-start.12
  909.7 227.4 %copy-start.24 = (s32[64]{0:T(128)S(1)}, s32[64]{0:T(128)}, u32[]{:S(2)}) copy-start(s32[64]{0:T(128)} %param.21) | copy-start | bytes 772
  909.8 228.7 %copy-start.11 = (f32[384,1024]{1,0:T(8,128)S(1)}, f32[384,1024]{1,0:T(8,128)}, u32[]{:S(2)}) copy-start(f32[384,1024]{1,0:T(8,128)} %param.30) | copy-start | bytes 4718596
  909.8 225.7 %all-reduce.5.cloned.1.call-start = ((), (), s32[]{:S(2)}) async-start(), calls=%async_computation.13 | async-start | bytes 524288 | tf_op jit(solution)/shard_map/psum | solution.py:190
  991.7 210.6 %copy-start.10 = (bf16[2048,256]{1,0:T(8,128)(2,1)}, bf16[2048,256]{1,0:T(8,128)(2,1)S(1)}, u32[]{:S(2)}) copy-start(bf16[2048,256]{1,0:T(8,128)(2,1)S(1)} %add_convert_fusion) | copy-start | bytes 3145732
  (24 other events, 50.6 us)
Sparse Core Ops, SparseCore 0:
  12.0 70.7 all-gather.3
  119.1 62.6 all-gather.5
  484.2 72.7 all-gather.7
  993.3 142.1 all-reduce.4
Sparse Core Ops, SparseCore 1:
  670.8 202.9 all-reduce.2
  909.9 79.6 reduce-scatter.1
where the time goes:
time: 1220 us; the launch traced here: 1210 us
  blocking collectives  418 us (34%)
  waiting for transfers between devices  406 us (33%)
  matrix products  127 us (10%)
  starting transfers between devices  91.3 us (7%)
  local copies, waits for them, and re-layouts  80.1 us (7%)
  other arithmetic  59.5 us (5%)
  between operations  16 us (1%)
    psum x1, waiting for transfers between devices, body(): last = lax.psum(placed, ('req', 'tp'))  142 us
    all_gather x1, blocking collectives, body(): lax.all_gather(served[3], 'req', axis=0, tiled=True)  115 us
    psum x1, waiting for transfers between devices, body(): summed = lax.psum(attn_part, 'tp')  95.2 us
    all_gather x1, blocking collectives, body(): lax.all_gather(served[1], 'req', axis=0, tiled=True)  85.3 us
    reduce_scatter x1, waiting for transfers between devices, body(): lax.psum_scatter(down_part, 'tp', scatter_dimension=1, tiled=True)  79.1 us
    all_gather x1, blocking collectives, body(): lax.all_gather(served[2], 'req', axis=0, tiled=True)  78.2 us
    all_gather x1, blocking collectives, body(): lax.all_gather(served[0], 'req', axis=0, tiled=True)  76.5 us
    pmax x1, blocking collectives, body(): top_logit = lax.pmax(jnp.max(logits, axis=-1), ('req', 'tp'))  63.4 us
  transfers between devices with their start and end apart: 15, of which 8 were waited for; matrix products, arithmetic and copies ran while one was open for 18% of the time, Pallas kernels for 0%

commit v1 on v0

--- a/solution.py
+++ b/solution.py
@@ -7,6 +7,12 @@
 HEAD_DIM = 64
 THETA = 160000.0
 EPS = 1e-05
+
+
+def summed_here(array, axis):
+    parts = lax.all_gather(array, axis, axis=0, tiled=False)
+    result = parts.sum(axis=0)
+    return result
 
 
 def with_halo(block, sides, width):
@@ -167,7 +173,7 @@
     attn_part = lax.dot_general(
         mixed, out_w, (((1,), (1,)), ((), ())), preferred_element_type=jnp.float32
     )
-    summed = lax.psum(attn_part, "tp")
+    summed = summed_here(attn_part, "tp")
     first = (hidden_in.astype(jnp.float32) + summed).astype(jnp.bfloat16)
     normed2 = layer_norm(first.astype(jnp.float32), mlp_gain).astype(jnp.bfloat16)
     first_share = lax.dynamic_slice_in_dim(first, tp_index * share, share, 1)

time: 1220 us -> 1360 us (1.11)
  waiting for transfers between devices: 406 us -> 532 us
  other arithmetic: 59.5 us -> 76 us
    all_gather x0 -> x1, waiting for transfers between devices: none -> 226 us  [summed_here(): parts = lax.all_gather(array, axis, axis=0, tiled=False)]
    psum x1 -> x0, waiting for transfers between devices: 95.2 us -> none  [body(): summed = lax.psum(attn_part, 'tp')]
    reduce_sum x0 -> x1, other arithmetic: none -> 16.5 us  [summed_here(): result = parts.sum(axis=0)]
  transfers between devices with their start and end apart: 15 -> 15, of which waited for: 8 -> 8; matrix products, arithmetic and copies ran while one was open for 18% -> 16% of each run, Pallas kernels for 0% -> 0%
where the time goes in v1:
time: 1360 us; the launch traced here: 1350 us
  waiting for transfers between devices  532 us (39%)
  blocking collectives  419 us (31%)
  matrix products  127 us (9%)
  starting transfers between devices  90.9 us (7%)
  local copies, waits for them, and re-layouts  80.1 us (6%)
  other arithmetic  76 us (6%)
  between operations  14.9 us (1%)
    all_gather x1, waiting for transfers between devices, summed_here(): parts = lax.all_gather(array, axis, axis=0, tiled=False)  226 us
    psum x1, waiting for transfers between devices, body(): last = lax.psum(placed, ('req', 'tp'))  143 us
    all_gather x1, blocking collectives, body(): lax.all_gather(served[3], 'req', axis=0, tiled=True)  115 us
    all_gather x1, blocking collectives, body(): lax.all_gather(served[1], 'req', axis=0, tiled=True)  85.3 us
    reduce_scatter x1, waiting for transfers between devices, body(): lax.psum_scatter(down_part, 'tp', scatter_dimension=1, tiled=True)  80.5 us
    all_gather x1, blocking collectives, body(): lax.all_gather(served[2], 'req', axis=0, tiled=True)  78.2 us
    all_gather x1, blocking collectives, body(): lax.all_gather(served[0], 'req', axis=0, tiled=True)  76.6 us
    pmax x1, blocking collectives, body(): top_logit = lax.pmax(jnp.max(logits, axis=-1), ('req', 'tp'))  63.4 us
  transfers between devices with their start and end apart: 15, of which 8 were waited for; matrix products, arithmetic and copies ran while one was open for 16% of the time, Pallas kernels for 0%

profile of v1, /device:TPU:1, one launch (start us, length us, event | category | flops | bytes accessed | tf_op | source)
XLA Modules:
  0.0 1349.7 jit_solution(18030433842945099375)
XLA Ops:
  9.6 85.3 %all_gather.28 = bf16[256,1024]{1,0:T(8,128)(2,1)S(1)} all-gather(bf16[8,1024]{1,0:T(8,128)(2,1)S(1)} %convert_element_type.94), channel_id=1, replica_groups=mesh['req'=32,'tp'=4] {'req'}, dimensions={0}, use_global_device_ids=true | all-gather | bytes 540672 | tf_op jit(solution)/shard_map/all_gather | solution.py:96
  95.9 18.5 %all-to-all-start.1 = ((bf16[256,4,256]{0,2,1:T(8,128)(2,1)}), bf16[256,4,256]{0,2,1:T(8,128)(2,1)S(1)}, u32[]{:S(2)}, u32[]{:S(2)}) async-start(bf16[256,4,256]{0,2,1:T(8,128)(2,1)} %bitcast.18), calls=%async_computation.1 | async-start | bytes 1048576 | tf_op jit(solution)/shard_map/all_to_all | solution.py:105
  123.2 76.6 %all_gather.27 = bf16[256,1024]{1,0:T(8,128)(2,1)S(1)} all-gather(bf16[8,1024]{1,0:T(8,128)(2,1)S(1)} %convert_element_type.92), channel_id=1, replica_groups=mesh['req'=32,'tp'=4] {'req'}, dimensions={0}, use_global_device_ids=true | all-gather | bytes 540672 | tf_op jit(solution)/shard_map/all_gather | solution.py:95
  199.8 78.2 %all_gather.29 = bf16[256,1024]{1,0:T(8,128)(2,1)S(1)} all-gather(bf16[8,1024]{1,0:T(8,128)(2,1)S(1)} %convert_element_type.96), channel_id=1, replica_groups=mesh['req'=32,'tp'=4] {'req'}, dimensions={0}, use_global_device_ids=true | all-gather | bytes 540672 | tf_op jit(solution)/shard_map/all_gather | solution.py:97
  278.3 4.3 fusion.12
  284.9 31.4 %all-to-all-start = ((bf16[256,4,256]{0,2,1:T(8,128)(2,1)}), bf16[256,4,256]{0,2,1:T(8,128)(2,1)S(1)}, u32[]{:S(2)}, u32[]{:S(2)}) async-start(bf16[256,4,256]{0,2,1:T(8,128)(2,1)} %bitcast.7), calls=%async_computation | async-start | bytes 1048576 | tf_op jit(solution)/shard_map/all_to_all | solution.py:104
  318.4 5.9 all-to-all-done
  324.3 4.8 all-to-all-start.2
  346.5 114.9 %all_gather.30 = bf16[256,1024]{1,0:T(8,128)(2,1)S(1)} all-gather(bf16[8,1024]{1,0:T(8,128)(2,1)S(1)} %convert_element_type.102), channel_id=1, replica_groups=mesh['req'=32,'tp'=4] {'req'}, dimensions={0}, use_global_device_ids=true | all-gather | bytes 540672 | tf_op jit(solution)/shard_map/all_gather | solution.py:98
  462.4 17.3 %all-to-all-start.3 = ((bf16[256,4,256]{0,2,1:T(8,128)(2,1)}), bf16[256,4,256]{0,2,1:T(8,128)(2,1)S(1)}, u32[]{:S(2)}, u32[]{:S(2)}) async-start(bf16[256,4,256]{0,2,1:T(8,128)(2,1)} %bitcast.36), calls=%async_computation.3 | async-start | bytes 1048576 | tf_op jit(solution)/shard_map/all_to_all | solution.py:107
  481.0 6.9 all-to-all-done.3
  495.9 4.8 copy.103
  503.9 159.8 %while.21 = (s32[]{:T(128)}, bf16[4,2048,64]{1,2,0:T(8,128)(2,1)}, bf16[4,2048,64]{1,2,0:T(8,128)(2,1)}, bf16[4,6144,64]{1,2,0:T(8,128)(2,1)}, bf16[4,6144,64]{1...) while((s32[]{:T(128)}, bf16[4,2048,64]{1,2,0:T(8,128)(2,1)}, ...), condition=%wide.region_11.12_spmd, body=%wide.region_6.0_spmd.sunk | while | flops 833616896 | bytes 53257172 | solution.py:171
  509.0 33.6 %while.22 = (s32[]{:T(128)}, bf16[4,512,64]{1,2,0:T(8,128)(2,1)S(1)}, s32[4]{0:T(128)S(1)}, s32[2048]{0:T(1024)S(1)}, s32[6144]{0:T(1024)S(1)}, /*index=5*/bf16[...) while((s32[]{:T(128)}, ...), condition=%wide.region_10.10_spmd, body=%wide.region_7.9_spmd.sunk | while | flops 833616896 | bytes 44343512 | solution.py:168
  548.9 33.6 %while.22 = (s32[]{:T(128)}, bf16[4,512,64]{1,2,0:T(8,128)(2,1)S(1)}, s32[4]{0:T(128)S(1)}, s32[2048]{0:T(1024)S(1)}, s32[6144]{0:T(1024)S(1)}, /*index=5*/bf16[...) while((s32[]{:T(128)}, ...), condition=%wide.region_10.10_spmd, body=%wide.region_7.9_spmd.sunk | while | flops 833616896 | bytes 44343512 | solution.py:168
  588.9 33.6 %while.22 = (s32[]{:T(128)}, bf16[4,512,64]{1,2,0:T(8,128)(2,1)S(1)}, s32[4]{0:T(128)S(1)}, s32[2048]{0:T(1024)S(1)}, s32[6144]{0:T(1024)S(1)}, /*index=5*/bf16[...) while((s32[]{:T(128)}, ...), condition=%wide.region_10.10_spmd, body=%wide.region_7.9_spmd.sunk | while | flops 833616896 | bytes 44343512 | solution.py:168
  628.8 33.6 %while.22 = (s32[]{:T(128)}, bf16[4,512,64]{1,2,0:T(8,128)(2,1)S(1)}, s32[4]{0:T(128)S(1)}, s32[2048]{0:T(1024)S(1)}, s32[6144]{0:T(1024)S(1)}, /*index=5*/bf16[...) while((s32[]{:T(128)}, ...), condition=%wide.region_10.10_spmd, body=%wide.region_7.9_spmd.sunk | while | flops 833616896 | bytes 44343512 | solution.py:168
  663.6 5.9 fusion.69
  672.1 4.4 all-to-all-start.4
  679.0 14.2 %all-to-all-done.4 = bf16[256,4,656]{0,2,1:T(8,128)(2,1)S(1)} async-done(((bf16[256,4,656]{0,2,1:T(8,128)(2,1)}), bf16[256,4,656]{0,2,1:T(8,128)(2,1)S(1)}, u32[]{:S(2)}, u32[]{:S(2)}) %all-to-all-start.4) | async-done | bytes 1343520 | tf_op jit(solution)/shard_map/all_to_all | solution.py:108
  693.2 4.5 all-to-all-start.5
  700.6 28.4 %all-to-all-done.5 = bf16[256,4,656]{0,2,1:T(8,128)(2,1)S(1)} async-done(((bf16[256,4,656]{0,2,1:T(8,128)(2,1)}), bf16[256,4,656]{0,2,1:T(8,128)(2,1)S(1)}, u32[]{:S(2)}, u32[]{:S(2)}) %all-to-all-start.5) | async-done | bytes 1343520 | tf_op jit(solution)/shard_map/all_to_all | solution.py:109
  729.0 5.2 all-to-all-start.6
  739.5 26.2 %all-to-all-done.6 = bf16[256,4,656]{0,2,1:T(8,128)(2,1)} async-done(((bf16[256,4,656]{0,2,1:T(8,128)(2,1)}), bf16[256,4,656]{0,2,1:T(8,128)(2,1)}, u32[]{:S(2)}, u32[]{:S(2)}) %all-to-all-start.6) | async-done | bytes 1343520 | tf_op jit(solution)/shard_map/all_to_all | solution.py:110
  769.3 226.1 %all-gather.12.cloned.1.call-done = f32[8192,1024]{1,0:T(8,128)} async-done(((f32[2048,1024]{1,0:T(8,128)}), f32[8192,1024]{1,0:T(8,128)}) %all-gather.12.cloned.1.call-update) | async-done | bytes 33554448 | tf_op jit(solution)/shard_map/all_gather | solution.py:13
  995.4 16.5 %reduce_sum.98 = f32[2048,1024]{1,0:T(8,128)} reduce(f32[4,2048,1024]{2,1,0:T(8,128)} %bitcast.108, f32[]{:T(128)} %constant.79.clone.1), dimensions={0}, to_apply=%region_12.13 | reduce | flops 6291456 | bytes 41943044 | tf_op jit(solution)/shard_map/reduce_sum | solution.py:14
  1011.9 5.5 convert_reduce_fusion.1
  1019.4 5.4 fusion.65
  1024.8 23.0 %fusion.30 = f32[2048,1024]{1,0:T(8,128)} fusion(f32[2048,656]{0,1:T(8,128)} %fusion.65, bf16[128,8,656]{2,1,0:T(8,128)(2,1)} %gather_fusion.7, bf16[128,8,656]{2,1,0:T(8,128)(2,1)S(1)} %copy-done.12, bf16[2048,1024]{1,0:T(8,128)(2,1)} %copy-done.5, f32[1024]{0:T(1024)S(1)} %copy-done.25, f32[2048]{0:T(1024)S(1)} %get-tuple-element.173, ...), kind=kOutput, calls=%fused_computation.64 | convolution fusion | flops 5602082816 | bytes 20664320 | tf_op jit(solution)/shard_map/dot_general | solution.py:183
  1048.5 80.5 %reduce-scatter.2.cloned.1.call-done = f32[2048,256]{1,0:T(8,128)} async-done(((f32[2048,1024]{1,0:T(8,128)}), f32[2048,256]{1,0:T(8,128)}) %reduce-scatter.2.cloned.1.call-update) | async-done | bytes 2097168 | tf_op jit(solution)/shard_map/reduce_scatter | solution.py:186
  1132.6 143.3 %all-reduce.2.cloned.1.call-done = f32[64,1024]{1,0:T(8,128)} async-done(((f32[64,1024]{1,0:T(8,128)}), f32[64,1024]{1,0:T(8,128)}) %all-reduce.2.cloned.1.call-update) | async-done | bytes 262160 | tf_op jit(solution)/shard_map/psum | solution.py:196
  1279.2 63.4 %pmax.7 = f32[64]{0:T(128)} all-reduce(f32[64]{0:T(128)S(1)} %convolution_reduce_fusion), channel_id=1, replica_groups=mesh['req'=32,'tp'=4] {'req','tp'}, use_global_device_ids=true, to_apply=%region_20.21 | all-reduce | flops 64 | bytes 512 | tf_op jit(solution)/shard_map/pmax | solution.py:211
  (297 shorter events, 222.6 us)
Async XLA Ops:
  7.2 1270.3 %copy-start = (f32[4,1024]{1,0:T(4,128)S(1)}, f32[4,1024]{1,0:T(4,128)}, u32[]{:S(2)}) copy-start(f32[4,1024]{1,0:T(4,128)} %param.33) | copy-start | bytes 49156
  7.2 113.7 %copy-start.1 = (s32[128]{0:T(128)S(1)}, s32[128]{0:T(128)}, u32[]{:S(2)}) copy-start(s32[128]{0:T(128)} %param.22) | copy-start | bytes 1540
  7.2 115.9 %copy-start.15 = (f32[8,1024]{1,0:T(8,128)S(1)}, f32[8,1024]{1,0:T(8,128)}, u32[]{:S(2)}) copy-start(f32[8,1024]{1,0:T(8,128)} %param.23) | copy-start | bytes 98308
  7.2 192.6 %copy-start.16 = (f32[8,1024]{1,0:T(8,128)S(1)}, f32[8,1024]{1,0:T(8,128)}, u32[]{:S(2)}) copy-start(f32[8,1024]{1,0:T(8,128)} %param.25) | copy-start | bytes 98308
  7.2 271.1 %copy-start.21 = (f32[1024]{0:T(1024)S(1)}, f32[1024]{0:T(1024)}, u32[]{:S(2)}) copy-start(f32[1024]{0:T(1024)} %param.31) | copy-start | bytes 12292
  7.2 662.4 %all-gather.6.cloned.1.call-start = ((), (), s32[]{:S(2)}) async-start(), calls=%async_computation.8 | async-start | bytes 1419264 | tf_op jit(solution)/shard_map/all_gather | solution.py:99
  95.9 189.0 %all-to-all-start.1 = ((bf16[256,4,256]{0,2,1:T(8,128)(2,1)}), bf16[256,4,256]{0,2,1:T(8,128)(2,1)S(1)}, u32[]{:S(2)}, u32[]{:S(2)}) async-start(bf16[256,4,256]{0,2,1:T(8,128)(2,1)} %bitcast.18), calls=%async_computation.1 | async-start | bytes 1048576 | tf_op jit(solution)/shard_map/all_to_all | solution.py:105
  114.4 562.1 %all-gather.8.cloned.1.call-start = ((), (), s32[]{:S(2)}) async-start(), calls=%async_computation.9 | async-start | bytes 1419264 | tf_op jit(solution)/shard_map/all_gather | solution.py:100
  117.4 363.3 %copy-start.19 = (s32[64]{0:T(128)}, s32[64]{0:T(128)S(1)}, u32[]{:S(2)}) copy-start(s32[64]{0:T(128)S(1)} %get-tuple-element.126) | copy-start | bytes 772
  123.1 365.0 %copy-start.18 = (s32[1024]{0:T(1024)}, s32[1024]{0:T(1024)S(1)}, u32[]{:S(2)}) copy-start(s32[1024]{0:T(1024)S(1)} %pad_clamp_fusion.1) | copy-start | bytes 12292
  278.3 6.4 copy-start.22
  284.9 39.4 %all-to-all-start = ((bf16[256,4,256]{0,2,1:T(8,128)(2,1)}), bf16[256,4,256]{0,2,1:T(8,128)(2,1)S(1)}, u32[]{:S(2)}, u32[]{:S(2)}) async-start(bf16[256,4,256]{0,2,1:T(8,128)(2,1)} %bitcast.7), calls=%async_computation | async-start | bytes 1048576 | tf_op jit(solution)/shard_map/all_to_all | solution.py:104
  324.3 13.3 all-to-all-start.2
  338.4 8.0 copy-start.17
  341.9 137.8 %copy-start.14 = (f32[8,2624]{1,0:T(8,128)S(1)}, f32[8,2624]{1,0:T(8,128)}, u32[]{:S(2)}) copy-start(f32[8,2624]{1,0:T(8,128)} %param.29) | copy-start | bytes 251908
  342.1 147.4 %copy-start.9 = (bf16[2,2048,256]{2,1,0:T(8,128)(2,1)}, bf16[2,2048,256]{2,1,0:T(8,128)(2,1)S(1)}, u32[]{:S(2)}) copy-start(bf16[2,2048,256]{2,1,0:T(8,128)(2,1)S(1)} %pad_maximum_fusion.1) | copy-start | bytes 6291460
  342.1 147.4 %collective-permute-start = (bf16[2,2048,256]{2,1,0:T(8,128)(2,1)S(1)}, bf16[2,2048,256]{2,1,0:T(8,128)(2,1)}, u32[]{:S(2)}, u32[]{:S(2)}) collective-permute-start(bf16[2,2048,256]{2,1,0:T(8,128)(2,1)S(1)} %pad_maximum_fusion.1), channel_id=1, source_target_pairs={{0,4},{4,8},{8,12},{12,16},{16,20},{20,24},{24,28},{28,32},{32,36}... | collective-permute-start | bytes 6291464 | tf_op jit(solution)/shard_map/ppermute | solution.py:23
  345.2 144.4 %collective-permute-start.1 = (bf16[2,2048,256]{2,1,0:T(8,128)(2,1)S(1)}, bf16[2,2048,256]{2,1,0:T(8,128)(2,1)}, u32[]{:S(2)}, u32[]{:S(2)}) collective-permute-start(bf16[2,2048,256]{2,1,0:T(8,128)(2,1)S(1)} %pad_maximum_fusion.1), channel_id=1, source_target_pairs={{4,0},{8,4},{12,8},{16,12},{20,16},{24,20},{28,24},{32,28},{36,32}... | collective-permute-start | bytes 6291464 | tf_op jit(solution)/shard_map/ppermute | solution.py:26
  462.4 25.5 %all-to-all-start.3 = ((bf16[256,4,256]{0,2,1:T(8,128)(2,1)}), bf16[256,4,256]{0,2,1:T(8,128)(2,1)S(1)}, u32[]{:S(2)}, u32[]{:S(2)}) async-start(bf16[256,4,256]{0,2,1:T(8,128)(2,1)} %bitcast.36), calls=%async_computation.3 | async-start | bytes 1048576 | tf_op jit(solution)/shard_map/all_to_all | solution.py:107
  479.7 218.0 %all-gather.10.cloned.1.call-start = ((), (), s32[]{:S(2)}) async-start(), calls=%async_computation.10 | async-start | bytes 1419264 | tf_op jit(solution)/shard_map/all_gather | solution.py:101
  480.5 514.9 %all-gather.12.cloned.1.call-start = ((), (), s32[]{:S(2)}) async-start(), calls=%async_computation.13 | async-start | bytes 41943040 | tf_op jit(solution)/shard_map/all_gather | solution.py:13
  672.1 21.1 %all-to-all-start.4 = ((bf16[256,4,656]{0,2,1:T(8,128)(2,1)}), bf16[256,4,656]{0,2,1:T(8,128)(2,1)S(1)}, u32[]{:S(2)}, u32[]{:S(2)}) async-start(bf16[256,4,656]{0,2,1:T(8,128)(2,1)} %bitcast.41), calls=%async_computation.4 | async-start | bytes 2686976 | tf_op jit(solution)/shard_map/all_to_all | solution.py:108
  693.2 35.7 %all-to-all-start.5 = ((bf16[256,4,656]{0,2,1:T(8,128)(2,1)}), bf16[256,4,656]{0,2,1:T(8,128)(2,1)S(1)}, u32[]{:S(2)}, u32[]{:S(2)}) async-start(bf16[256,4,656]{0,2,1:T(8,128)(2,1)} %bitcast.118), calls=%async_computation.5 | async-start | bytes 2686976 | tf_op jit(solution)/shard_map/all_to_all | solution.py:109
  729.0 5.5 copy-start.6
  729.0 36.8 %all-to-all-start.6 = ((bf16[256,4,656]{0,2,1:T(8,128)(2,1)}), bf16[256,4,656]{0,2,1:T(8,128)(2,1)}, u32[]{:S(2)}, u32[]{:S(2)}) async-start(bf16[256,4,656]{0,2,1:T(8,128)(2,1)} %bitcast.117), calls=%async_computation.6 | async-start | bytes 2686976 | tf_op jit(solution)/shard_map/all_to_all | solution.py:110
  734.2 394.8 %reduce-scatter.2.cloned.1.call-start = ((), (), s32[]{:S(2)}) async-start(), calls=%async_computation.11 | async-start | bytes 10485760 | tf_op jit(solution)/shard_map/reduce_scatter | solution.py:186
  1011.9 7.5 copy-start.25
  1019.4 5.4 copy-start.12
  1047.8 229.7 %copy-start.24 = (s32[64]{0:T(128)S(1)}, s32[64]{0:T(128)}, u32[]{:S(2)}) copy-start(s32[64]{0:T(128)} %param.21) | copy-start | bytes 772
  1047.8 231.0 %copy-start.11 = (f32[384,1024]{1,0:T(8,128)S(1)}, f32[384,1024]{1,0:T(8,128)}, u32[]{:S(2)}) copy-start(f32[384,1024]{1,0:T(8,128)} %param.30) | copy-start | bytes 4718596
  1047.8 228.1 %all-reduce.2.cloned.1.call-start = ((), (), s32[]{:S(2)}) async-start(), calls=%async_computation.12 | async-start | bytes 524288 | tf_op jit(solution)/shard_map/psum | solution.py:196
  1131.1 211.5 %copy-start.10 = (bf16[2048,256]{1,0:T(8,128)(2,1)}, bf16[2048,256]{1,0:T(8,128)(2,1)S(1)}, u32[]{:S(2)}) copy-start(bf16[2048,256]{1,0:T(8,128)(2,1)S(1)} %add_convert_fusion) | copy-start | bytes 3145732
  (24 other events, 50.7 us)
Sparse Core Ops, SparseCore 0:
  11.1 70.7 all-gather.5
  118.3 62.2 all-gather.7
  483.6 72.6 all-gather.9
  669.7 325.6 all-gather.11
  1047.9 81.0 reduce-scatter.1
  1133.6 142.2 all-reduce.1
